TPU v7x, 32 devices: a whole 2x2x4 slice. The times are simulated.
32 devices in a mesh: dp: 8 (over y, x, core), seq: 4 (over z).
Axes of the slice: x: 2, y: 2, z: 4, core: 2. Of those that a mesh axis runs over, the one named last changes fastest.
Arguments:
- tokens: bfloat16 [8, 1024, 1280], P('dp', 'seq'), may hold values from -6 to 6
- tube_index: int32 [8, 1024], P('dp', 'seq'), may hold values from 0 to 16383
- counts: int32 [8, 4], P('dp', 'seq'), may hold values from 128 to 256
- qkv_weight: bfloat16 [1280, 3840], P('dp'), may hold values from -4 to 4
- proj_weight: bfloat16 [1280, 1280], P('dp'), may hold values from -0.15625 to 0.15625
- ctx_b: bfloat16 [8, 1024, 1280], P('dp', 'seq'), may hold values from -12 to 12
- cot_b: bfloat16 [8, 1024, 1280], P('dp', 'seq'), may hold values from -12 to 12
- b_counts: int32 [8, 4], P('dp', 'seq'), may hold values from 128 to 256
Outputs:
- out_a: bfloat16 [8, 1024, 1280], P('dp', 'seq')
- weight_grad: float32 [1280, 1280], P('dp')
Inputs may be any that keep to these rules, and one draw needn't show every extreme that they name: `counts`: slots of a device's block past its count hold padding. `b_counts`: slots of a device's block past its count hold padding.
All inputs are finite; a program needn't handle non-finite values.
Results may differ from a plain program's by a relative error of at most 0.017.
Values may be sent and summed in bfloat16 or wider, within the bound.
A program may use at most 128 MiB of HBM per device.

v0:
```python
import math

import jax
import jax.numpy as jnp
from jax import lax
from jax.sharding import PartitionSpec as P

HEADS = 16


def embed(tube_ids, model_width):
    half_width = model_width // 2
    positions = jnp.arange(half_width, dtype=jnp.float32)
    frequency = jnp.exp(positions * (-2.0 * math.log(10000.0) / model_width))
    angles = tube_ids.astype(jnp.float32)[:, None] * frequency[None, :]
    return jnp.concatenate([jnp.sin(angles), jnp.cos(angles)], axis=1)


def layer_norm(values):
    centered = values - jnp.mean(values, axis=1, keepdims=True)
    spread = jnp.mean(centered * centered, axis=1, keepdims=True)
    return centered * lax.rsqrt(spread + 1e-06)


def attend(grouped, valid_keys, heads_here, head_width):
    seq_length = grouped.shape[0]
    query_rows = grouped[:, 0].reshape(seq_length, heads_here, head_width)
    key_rows = grouped[:, 1].reshape(seq_length, heads_here, head_width)
    value_rows = grouped[:, 2].reshape(seq_length, heads_here, head_width)
    block_rows = math.gcd(seq_length, 512)
    score_scale = 1.0 / math.sqrt(head_width)
    blocked = query_rows.reshape(seq_length // block_rows, block_rows, heads_here, head_width)

    def one_block(block_query):
        scores = (
            jnp.einsum("qhd,khd->hqk", block_query, key_rows, preferred_element_type=jnp.float32)
            * score_scale
        )
        scores = jnp.where(valid_keys[None, None, :], scores, -1e30)
        top_score = jnp.max(scores, axis=2, keepdims=True)
        exponent = jnp.exp(scores - top_score)
        weights = (exponent / jnp.sum(exponent, axis=2, keepdims=True)).astype(jnp.bfloat16)
        return jnp.einsum(
            "hqk,khd->qhd", weights, value_rows, preferred_element_type=jnp.float32
        ).astype(jnp.bfloat16)

    return lax.map(one_block, blocked).reshape(seq_length, heads_here * head_width)


def on_device(tokens, tube_index, counts, qkv_weight, proj_weight, ctx_b, cot_b, b_counts):
    slot_cap = tokens.shape[1]
    model_width = tokens.shape[2]
    seq_count = lax.axis_size("seq")
    dp_count = lax.axis_size("dp")
    heads_here = HEADS // seq_count
    head_width = model_width // HEADS
    with_pos = tokens[0].astype(jnp.float32) + embed(tube_index[0], model_width)
    normed = layer_norm(with_pos).astype(jnp.bfloat16)
    columns = normed
    projected = jnp.dot(
        columns,
        lax.all_gather(qkv_weight, "dp", axis=0, tiled=True),
        preferred_element_type=jnp.float32,
    ).astype(jnp.bfloat16)
    all_counts = lax.all_gather(counts, "seq", axis=1, tiled=True)
    slot_ids = lax.broadcasted_iota(jnp.int32, (1, slot_cap), 1)
    valid_keys = (slot_ids < all_counts[0][:, None]).reshape(seq_count * slot_cap)
    grouped = lax.all_to_all(
        projected.reshape(slot_cap, 3, model_width), "seq", split_axis=2, concat_axis=0, tiled=True
    )
    head_context = attend(grouped, valid_keys, heads_here, head_width)
    context = lax.all_to_all(head_context, "seq", split_axis=0, concat_axis=1, tiled=True)
    columns = context
    mixed = jnp.dot(
        columns,
        lax.all_gather(proj_weight, "dp", axis=0, tiled=True),
        preferred_element_type=jnp.float32,
    )
    out_a = (with_pos + mixed).astype(jnp.bfloat16)[None]
    row_ids = lax.broadcasted_iota(jnp.int32, (slot_cap, 1), 0)
    keep_rows = row_ids < b_counts[0, 0]
    masked_cot = jnp.where(keep_rows, cot_b[0], jnp.zeros((), jnp.bfloat16))
    factor = 1.0 / math.sqrt(dp_count * seq_count * slot_cap)
    column_part = ctx_b[0]
    own_rows = lax.psum_scatter(
        lax.dot_general(
            column_part, masked_cot, (((0,), (0,)), ((), ())), preferred_element_type=jnp.float32
        )
        * factor,
        "dp",
        scatter_dimension=0,
        tiled=True,
    )
    weight_grad = lax.psum(own_rows.astype(jnp.bfloat16), "seq").astype(jnp.float32)
    return (out_a, weight_grad)


def solution(mesh):
    in_specs = (
        P("dp", "seq", None),
        P("dp", "seq"),
        P("dp", "seq"),
        P("dp", None),
        P("dp", None),
        P("dp", "seq", None),
        P("dp", "seq", None),
        P("dp", "seq"),
    )
    out_specs = (P("dp", "seq", None), P("dp", None))
    return jax.shard_map(
        on_device, mesh=mesh, in_specs=in_specs, out_specs=out_specs, check_vma=False
    )
```

profile of v0, /device:TPU:0, one launch (start us, length us, event | category | flops | bytes accessed | tf_op | source)
XLA Modules:
  0.0 233.4 jit_solution(339706561410312037)
XLA Ops:
  7.2 0.7 all-gather.3.cloned.1.call-update
  8.6 5.0 %fusion.30 = f32[1280,1280]{0,1:T(8,128)} fusion(bf16[1,256,1280]{2,1,0:T(8,128)(2,1)S(1)} %copy-done, bf16[1,256,1280]{2,1,0:T(8,128)(2,1)} %param.16, pred[256]{0:T(512)(128)(4,1)S(1)} %iota_compare_fusion.1), kind=kOutput, calls=%fused_computation.25 | convolution fusion | flops 840826880 | bytes 7864576 | tf_op jit(solution)/shard_map/dot_general | solution.py:86
  13.6 8.2 %copy.31 = f32[1280,1280]{1,0:T(8,128)} copy(f32[1280,1280]{0,1:T(8,128)} %fusion.30) | data formatting | bytes 13107200
  22.6 2.3 %multiply_sine_fusion = (f32[256,640]{1,0:T(8,128)S(1)}, f32[256,640]{1,0:T(8,128)S(1)}) fusion(f32[640]{0:T(1024)S(1)} %multiply_exponential_fusion, f32[256]{0:T(256)S(1)} %bitcast.83), kind=kLoop, calls=%fused_computation.34 | loop fusion | flops 163840 | bytes 1314304 | tf_op jit(solution)/shard_map/sin | solution.py:16
  25.5 47.5 %all-gather.3.cloned.1.call-done = bf16[1280,3840]{1,0:T(8,128)(2,1)} async-done(((bf16[160,3840]{1,0:T(8,128)(2,1)}), bf16[1280,3840]{1,0:T(8,128)(2,1)}) %all-gather.3.cloned.1.call-update) | async-done | bytes 9830416 | tf_op jit(solution)/shard_map/all_gather | solution.py:62
  73.0 7.9 %convolution_convert_fusion = bf16[256,3840]{1,0:T(8,128)(2,1)} fusion(bf16[1280,3840]{1,0:T(8,128)(2,1)} %all-gather.3.cloned.1.call-done, f32[256]{0:T(256)S(1)} %add_rsqrt_fusion, f32[256]{0:T(256)S(1)} %broadcast_multiply_fusion, f32[256,640]{1,0:T(8,128)S(1)} %get-tuple-element.94, f32[256,640]{1,0:T(8,128)S(1)} %get-tuple-element.93, ...), kind=kOutput, calls=%fused_computation.26 | convolution fusion | flops 2519531520 | bytes 13764608 | tf_op jit(solution)/shard_map/dot_general | solution.py:60
  80.9 2.8 %copy.23 = bf16[256,3840]{0,1:T(8,128)(2,1)S(1)} copy(bf16[256,3840]{1,0:T(8,128)(2,1)} %convolution_convert_fusion) | data formatting | bytes 3932160 | tf_op jit(solution)/shard_map/convert_element_type | solution.py:64
  83.7 11.2 %copy.24 = bf16[256,3,1280]{0,1,2:T(4,128)(2,1)} copy(bf16[256,3,1280]{0,2,1:T(8,128)(2,1)S(1)} %bitcast.78) | data formatting | bytes 3932160 | tf_op jit(solution)/shard_map/reshape | solution.py:69
  94.9 4.5 %all-to-all-start = ((bf16[256,3,1280]{0,1,2:T(4,128)(2,1)}), bf16[256,3,1280]{0,1,2:T(4,128)(2,1)S(1)}, u32[]{:S(2)}, u32[]{:S(2)}) async-start(bf16[256,3,1280]{0,1,2:T(4,128)(2,1)} %copy.24), calls=%async_computation | async-start | bytes 5242880 | tf_op jit(solution)/shard_map/all_to_all | solution.py:68
  99.3 40.2 %reduce-scatter.4.cloned.1.call-done = f32[160,1280]{1,0:T(8,128)} async-done(((f32[1280,1280]{1,0:T(8,128)}), f32[160,1280]{1,0:T(8,128)}) %reduce-scatter.4.cloned.1.call-update) | async-done | bytes 819216
  139.5 2.2 copy.32
  144.2 25.7 %all-reduce = s32[4]{0:T(128)S(1)} all-reduce(s32[4]{0:T(128)S(1)} %bitcast_dynamic-update-slice_fusion), channel_id=1, replica_groups=mesh['dp'=8,'seq'=4] {'seq'}, use_global_device_ids=true, to_apply=%add | all-reduce | flops 4 | bytes 32
  170.5 1.0 fusion.47
  172.6 24.1 %while.11 = (s32[]{:T(128)}, bf16[2,512,4,80]{1,3,2,0:T(8,128)(2,1)S(1)}, bf16[2,512,4,80]{1,3,2,0:T(8,128)(2,1)S(1)}, bf16[1024,4,80]{0,2,1:T(8,128)(2,1)}, bf1...) while((s32[]{:T(128)}, bf16[2,512,4,80]{1,3,2,0:T(8,128)(2,1)S(1)}, ...), condition=%wide.region_5.6_spmd.clone, body=%wide.region_2.5_spmd.clone.sunk | while | flops 683837440 | bytes 18763876 | solution.py:47
  172.7 7.1 %fusion.62 = (f32[4,512]{1,0:T(4,128)S(1)}, f32[4,512,1024]{2,1,0:T(8,128)}) fusion(pred[1024]{0:T(1024)(128)(4,1)S(1)} %broadcast_in_dim.77, bf16[1024,4,80]{0,2,1:T(8,128)(2,1)} %get-tuple-element.153, bf16[2,512,4,80]{1,3,2,0:T(8,128)(2,1)S(1)} %get-tuple-element.152, s32[]{:T(128)} %get-tuple-element.143), kind=kOutput, calls=%fused_computation.49.clone.1 | convolution fusion | flops 343933952 | bytes 9380868 | tf_op jit(solution)/shard_map/while/body/eval_jaxpr/sub | solution.py:41
  179.7 4.9 %fusion.63 = bf16[2,512,4,80]{1,3,2,0:T(8,128)(2,1)S(1)} fusion(bf16[2,512,4,80]{1,3,2,0:T(8,128)(2,1)S(1)} %get-tuple-element.144, s32[]{:T(128)} %get-tuple-element.143, bf16[1024,4,80]{0,2,1:T(8,128)(2,1)S(1)} %get-tuple-element.154, f32[4,512,1024]{2,1,0:T(8,128)} %get-tuple-element.134, f32[4,512]{1,0:T(4,128)S(1)} %get-tuple-element.135), kind=kOutput, calls=%fused_computation.12.clone.1 | convolution fusion | flops 339902464 | bytes 9379844 | tf_op jit(solution)/shard_map/while/body/eval_jaxpr/hqk,khd->qhd/dot_general | solution.py:43
  184.7 7.1 %fusion.62 = (f32[4,512]{1,0:T(4,128)S(1)}, f32[4,512,1024]{2,1,0:T(8,128)}) fusion(pred[1024]{0:T(1024)(128)(4,1)S(1)} %broadcast_in_dim.77, bf16[1024,4,80]{0,2,1:T(8,128)(2,1)} %get-tuple-element.153, bf16[2,512,4,80]{1,3,2,0:T(8,128)(2,1)S(1)} %get-tuple-element.152, s32[]{:T(128)} %get-tuple-element.143), kind=kOutput, calls=%fused_computation.49.clone.1 | convolution fusion | flops 343933952 | bytes 9380868 | tf_op jit(solution)/shard_map/while/body/eval_jaxpr/sub | solution.py:41
  191.8 4.8 %fusion.63 = bf16[2,512,4,80]{1,3,2,0:T(8,128)(2,1)S(1)} fusion(bf16[2,512,4,80]{1,3,2,0:T(8,128)(2,1)S(1)} %get-tuple-element.144, s32[]{:T(128)} %get-tuple-element.143, bf16[1024,4,80]{0,2,1:T(8,128)(2,1)S(1)} %get-tuple-element.154, f32[4,512,1024]{2,1,0:T(8,128)} %get-tuple-element.134, f32[4,512]{1,0:T(4,128)S(1)} %get-tuple-element.135), kind=kOutput, calls=%fused_computation.12.clone.1 | convolution fusion | flops 339902464 | bytes 9379844 | tf_op jit(solution)/shard_map/while/body/eval_jaxpr/hqk,khd->qhd/dot_general | solution.py:43
  196.6 0.7 copy.28
  197.6 0.9 copy.29
  198.5 3.5 %all-to-all-start.1 = ((bf16[4,256,320]{1,2,0:T(8,128)(2,1)}), bf16[4,256,320]{1,2,0:T(8,128)(2,1)S(1)}, u32[]{:S(2)}, u32[]{:S(2)}) async-start(bf16[4,256,320]{1,2,0:T(8,128)(2,1)} %copy.29), calls=%async_computation.1 | async-start | bytes 1310720 | tf_op jit(solution)/shard_map/all_to_all | solution.py:72
  202.1 2.2 copy.30
  204.3 18.8 %all-gather.5.cloned.1.call-done = bf16[1280,1280]{1,0:T(8,128)(2,1)} async-done(((bf16[160,1280]{1,0:T(8,128)(2,1)}), bf16[1280,1280]{1,0:T(8,128)(2,1)}) %all-gather.5.cloned.1.call-update) | async-done | bytes 3276816 | tf_op jit(solution)/shard_map/all_gather | solution.py:76
  223.0 3.8 %fusion.32 = bf16[1,256,1280]{2,1,0:T(8,128)(2,1)} fusion(bf16[256,1280]{0,1:T(8,128)(2,1)S(1)} %bitcast.80, bf16[1280,1280]{1,0:T(8,128)(2,1)} %all-gather.5.cloned.1.call-done, f32[256,640]{1,0:T(8,128)S(1)} %copy-done.4, f32[256,640]{1,0:T(8,128)S(1)} %copy-done.2, bf16[1,256,1280]{2,1,0:T(8,128)(2,1)S(1)} %copy-done.6), kind=kOutput, calls=%fused_computation.29 | convolution fusion | flops 840499200 | bytes 6553600 | tf_op jit(solution)/shard_map/dot_general | solution.py:74
  (50 shorter events, 5.3 us)
Async XLA Ops:
  7.2 1.5 copy-start
  7.2 65.8 %all-gather.3.cloned.1.call-start = ((), (), s32[]{:S(2)}) async-start(), calls=%async_computation.3 | async-start | bytes 11059200 | tf_op jit(solution)/shard_map/all_gather | solution.py:62
  7.9 131.6 %reduce-scatter.4.cloned.1.call-start = ((), (), s32[]{:S(2)}) async-start(), calls=%async_computation.6 | async-start | bytes 7372800
  21.9 0.7 copy-start.8
  21.9 3.1 %copy-start.5 = (bf16[1,256,1280]{2,1,0:T(8,128)(2,1)S(1)}, bf16[1,256,1280]{2,1,0:T(8,128)(2,1)}, u32[]{:S(2)}) copy-start(bf16[1,256,1280]{2,1,0:T(8,128)(2,1)} %param.10) | copy-start | bytes 1966084
  24.9 48.1 %copy-start.1 = (f32[256,640]{1,0:T(8,128)}, f32[256,640]{1,0:T(8,128)S(1)}, u32[]{:S(2)}) copy-start(f32[256,640]{1,0:T(8,128)S(1)} %get-tuple-element.93) | copy-start | bytes 1966084
  24.9 48.1 %copy-start.3 = (f32[256,640]{1,0:T(8,128)}, f32[256,640]{1,0:T(8,128)S(1)}, u32[]{:S(2)}) copy-start(f32[256,640]{1,0:T(8,128)S(1)} %get-tuple-element.94) | copy-start | bytes 1966084
  94.9 75.1 %all-to-all-start = ((bf16[256,3,1280]{0,1,2:T(4,128)(2,1)}), bf16[256,3,1280]{0,1,2:T(4,128)(2,1)S(1)}, u32[]{:S(2)}, u32[]{:S(2)}) async-start(bf16[256,3,1280]{0,1,2:T(4,128)(2,1)} %copy.24), calls=%async_computation | async-start | bytes 5242880 | tf_op jit(solution)/shard_map/all_to_all | solution.py:68
  99.3 43.6 %copy-start.9 = (u32[32]{0:T(128)S(1)}, u32[32]{0:T(128)}, u32[]{:S(2)}) copy-start(u32[32]{0:T(128)} %constant.42) | copy-start | bytes 388
  99.3 102.7 %all-reduce.3.cloned.1.call-start = ((), (), s32[]{:S(2)}) async-start(), calls=%async_computation.5 | async-start | bytes 1310720 | tf_op jit(solution)/shard_map/psum | solution.py:94
  141.7 81.3 %all-gather.5.cloned.1.call-start = ((), (), s32[]{:S(2)}) async-start(), calls=%async_computation.4 | async-start | bytes 3686400 | tf_op jit(solution)/shard_map/all_gather | solution.py:76
  171.5 1.1 copy-start.7
  197.6 25.5 %copy-start.2 = (f32[256,640]{1,0:T(8,128)S(1)}, f32[256,640]{1,0:T(8,128)}, u32[]{:S(2)}) copy-start(f32[256,640]{1,0:T(8,128)} %copy-done.1) | copy-start | bytes 1966084
  197.6 25.4 %copy-start.4 = (f32[256,640]{1,0:T(8,128)S(1)}, f32[256,640]{1,0:T(8,128)}, u32[]{:S(2)}) copy-start(f32[256,640]{1,0:T(8,128)} %copy-done.3) | copy-start | bytes 1966084
  197.6 25.4 %copy-start.6 = (bf16[1,256,1280]{2,1,0:T(8,128)(2,1)S(1)}, bf16[1,256,1280]{2,1,0:T(8,128)(2,1)}, u32[]{:S(2)}) copy-start(bf16[1,256,1280]{2,1,0:T(8,128)(2,1)} %param.10) | copy-start | bytes 1966084
  198.5 24.5 %all-to-all-start.1 = ((bf16[4,256,320]{1,2,0:T(8,128)(2,1)}), bf16[4,256,320]{1,2,0:T(8,128)(2,1)S(1)}, u32[]{:S(2)}, u32[]{:S(2)}) async-start(bf16[4,256,320]{1,2,0:T(8,128)(2,1)} %copy.29), calls=%async_computation.1 | async-start | bytes 1310720 | tf_op jit(solution)/shard_map/all_to_all | solution.py:72
Sparse Core Ops, SparseCore 0:
  9.9 63.0 all-gather.2
  76.4 63.0 reduce-scatter.3
  141.9 47.0 all-reduce.2
  190.7 32.2 all-gather.4
where the time goes:
time: 234 us; the launch traced here: 233 us
  waiting for transfers between devices  108 us (46%)
  matrix products  40.5 us (17%)
  local copies, waits for them, and re-layouts  33.1 us (14%)
  blocking collectives  25.7 us (11%)
  between operations  15.2 us (6%)
  starting transfers between devices  8.06 us (3%)
  other arithmetic  3.06 us (1%)
    all_gather x1, waiting for transfers between devices, on_device(): lax.all_gather(qkv_weight, 'dp', axis=0, tiled=True)  47.5 us
    unnamed x5, waiting for transfers between devices  41.4 us
    unnamed x1, blocking collectives  25.7 us
    all_gather x1, waiting for transfers between devices, on_device(): lax.all_gather(proj_weight, 'dp', axis=0, tiled=True)  18.8 us
    unnamed x27, local copies, waits for them, and re-layouts  15.2 us
    sub x2, matrix products, one_block(): exponent = jnp.exp(scores - top_score)  14.2 us
    reshape x1, local copies, waits for them, and re-layouts, on_device(): projected.reshape(slot_cap, 3, model_width)  11.2 us
    dot_general x2, matrix products, one_block(): jnp.einsum('hqk,khd->qhd', weights, value_rows, preferred_element_type=jn...  9.71 us
  transfers between devices with their start and end apart: 6, of which 3 were waited for; matrix products, arithmetic and copies ran while one was open for 31% of the time, Pallas kernels for 0%

commit v1 on v0

v1 whole, which is shorter than its diff:
```python
import functools
import math

import jax
import jax.numpy as jnp
from jax import lax
from jax.experimental import pallas as pl
from jax.experimental.pallas import tpu as pltpu
from jax.sharding import PartitionSpec as P

HEADS = 16


def layer_norm(values):
    centered = values - jnp.mean(values, axis=1, keepdims=True)
    spread = jnp.mean(centered * centered, axis=1, keepdims=True)
    return centered * lax.rsqrt(spread + 1e-06)


LANES = 128
MESH = pl.DeviceIdType.MESH
LOG2_E = math.log2(math.e)


def round_up(value, unit):
    return (value + unit - 1) // unit * unit


def window(width, seq_count, head_cols):
    size = max(owner * head_cols % LANES + head_cols for owner in range(seq_count))
    size = round_up(size, LANES)
    return size, [min(owner * head_cols // LANES * LANES, width - size) for owner in range(seq_count)]


def block_kernel(
    dp_count, seq_count, heads_here, head_width,
    tok_ref, index_ref, freq_ref, count_ref, bcount_ref, w_ref, proj_ref, ctxb_ref, cot_ref,
    out_ref, grad_ref,
    x_all, bias_all, w_all, p_all, qkv, acc, ctx_send, ctx_all,
    g_part, g_sib, g_chip, g_recv, g_seq, pos, index_col, ctxb, cot,
    l_sems, xr_sems, xl_sems, bias_sems, w_sems, w_fsems, p_sems, p_fsems, c_sems, gs_sems, gr_sems,
    ar_sems, al_sems,
):
    d = lax.axis_index("dp")
    s = lax.axis_index("seq")
    core = lax.rem(d, 2)
    chip = lax.div(d, 2)
    chips = dp_count // 2
    sibling = chip * 2 + 1 - core
    slots, width = tok_ref.shape
    rows = w_ref.shape[0]
    head_cols = heads_here * head_width
    part, starts = window(width, seq_count, head_cols)
    offsets = [owner * head_cols - start for owner, start in enumerate(starts)]
    first_lane = lax.min(lax.div(s * head_cols, LANES) * LANES, width - part)
    offset = s * head_cols - first_lane

    def ahead(v):
        return lax.rem(chip + v, chips)

    def behind(v):
        return lax.rem(chip + chips - v, chips)

    def seq_ahead(k):
        return lax.rem(s + k, seq_count)

    def seq_behind(k):
        return lax.rem(s + seq_count - k, seq_count)

    def row_block(index):
        return pl.ds(pl.multiple_of(index * rows, rows), rows)

    def slot_block(index):
        return pl.ds(pl.multiple_of(index * slots, slots), slots)

    def to_dp(src, dst, sems, index, target):
        return pltpu.make_async_remote_copy(
            src_ref=src, dst_ref=dst, send_sem=sems.at[0, index], recv_sem=sems.at[1, index],
            device_id={"dp": target, "seq": s}, device_id_type=MESH,
        )

    def to_seq(src, dst, sems, index, target):
        return pltpu.make_async_remote_copy(
            src_ref=src, dst_ref=dst, send_sem=sems.at[0, index], recv_sem=sems.at[1, index],
            device_id={"dp": d, "seq": target}, device_id_type=MESH,
        )

    local = [
        pltpu.make_async_copy(
            w_ref.at[:, pl.ds(pl.multiple_of(kind * width + first_lane, LANES), part)],
            w_all.at[row_block(d), kind * part:(kind + 1) * part], l_sems.at[kind],
        )
        for kind in range(3)
    ]
    local.append(pltpu.make_async_copy(ctxb_ref, ctxb, l_sems.at[3]))
    local.append(pltpu.make_async_copy(cot_ref, cot, l_sems.at[4]))
    local.append(pltpu.make_async_copy(proj_ref, p_all.at[row_block(d)], l_sems.at[5]))
    for copy in local:
        copy.start()

    barrier = pltpu.get_barrier_semaphore()
    for v in range(1, chips):
        pl.semaphore_signal(barrier, inc=1, device_id={"dp": ahead(v) * 2 + core, "seq": s}, device_id_type=MESH)
    pl.semaphore_signal(barrier, inc=1, device_id={"dp": sibling, "seq": s}, device_id_type=MESH)
    for k in range(1, seq_count):
        pl.semaphore_signal(barrier, inc=1, device_id={"dp": d, "seq": seq_ahead(k)}, device_id_type=MESH)

    slot_ids = lax.broadcasted_iota(jnp.int32, (8, slots), 1)
    bias_all[:, slot_block(s)] = jnp.where(slot_ids < count_ref[...], 0.0, -1e30)
    index_col[...] = jnp.broadcast_to(index_ref[...].astype(jnp.float32), (8, slots)).T
    group = math.gcd(slots, 32)

    @pl.loop(0, slots // group)
    def _(j):
        span = pl.ds(pl.multiple_of(j * group, group), group)
        angles = index_col[span, 0:1] * freq_ref[...]
        shift = jnp.concatenate([jnp.sin(angles), jnp.cos(angles)], axis=1)
        with_pos = tok_ref[span, :].astype(jnp.float32) + shift
        pos[span, :] = with_pos
        own_span = pl.ds(pl.multiple_of(s * slots + j * group, group), group)
        x_all[own_span, :] = layer_norm(with_pos).astype(jnp.bfloat16)

    for copy in local[:3]:
        copy.wait()
    pl.semaphore_wait(barrier, chips - 1 + 1 + seq_count - 1)

    sends = []

    def start(copy):
        copy.start()
        sends.append(copy)

    right, left = seq_ahead(1), seq_behind(1)
    rounds = seq_count // 2

    def ring_piece(place, sems, step, origin, piece, target):
        block = place(origin, piece)
        return pltpu.make_async_remote_copy(
            src_ref=block, dst_ref=block, send_sem=sems.at[0, step, piece], recv_sem=sems.at[1, step, piece],
            device_id={"dp": d, "seq": target}, device_id_type=MESH,
        )

    def ring_start(place, r_sems, l_sems):
        for order in range(2):
            if order == 0 or rounds > 1:
                start(ring_piece(place, r_sems, 0, s, order, right))
                start(ring_piece(place, l_sems, 0, s, 1 - order, left))

    def ring_forward(place, r_sems, l_sems):
        for step in range(1, rounds):
            for order in range(2):
                ring_piece(place, r_sems, step - 1, seq_behind(step), order, right).wait_recv()
                if order == 0 or step < rounds - 1:
                    start(ring_piece(place, r_sems, step, seq_behind(step), order, right))
                ring_piece(place, l_sems, step - 1, seq_ahead(step), 1 - order, left).wait_recv()
                if order == 0 or step < rounds - 1:
                    start(ring_piece(place, l_sems, step, seq_ahead(step), 1 - order, left))

    def ring_finish(place, r_sems, l_sems):
        ring_piece(place, r_sems, rounds - 1, seq_behind(rounds), 0, right).wait_recv()
        ring_piece(place, l_sems, rounds - 1, seq_ahead(rounds), 1, left).wait_recv()

    def x_place(origin, piece):
        half_rows = slots // 2
        return x_all.at[pl.ds(pl.multiple_of(origin * slots + piece * half_rows, half_rows), half_rows)]

    def g_place(origin, piece):
        half_rows = rows // 2
        return g_seq.at[origin, pl.ds(piece * half_rows, half_rows)]

    own_w = w_all.at[row_block(d)]
    own_p = p_all.at[row_block(d)]
    for v in range(1, chips):
        start(to_dp(own_w, own_w, w_sems, v - 1, ahead(v) * 2 + core))
    ring_start(x_place, xr_sems, xl_sems)
    start(to_dp(own_w, own_w, w_fsems, 0, sibling))
    for k in range(1, seq_count):
        spot = bias_all.at[:, slot_block(s)]
        start(to_seq(spot, spot, bias_sems, k - 1, seq_ahead(k)))

    for copy in local[3:]:
        copy.wait()
    keep = lax.broadcasted_iota(jnp.int32, (slots, LANES), 0) < bcount_ref[...]
    keep = jnp.where(keep, 1.0, 0.0)[:, 0:1].astype(jnp.bfloat16)
    cot[...] = cot[...] * keep
    step = math.gcd(width, 256)

    @pl.loop(0, width // step)
    def _(j):
        span = pl.ds(pl.multiple_of(j * step, step), step)
        g_part[span, :] = lax.dot_general(
            ctxb[:, span], cot[...], (((0,), (0,)), ((), ())), preferred_element_type=jnp.float32
        ).astype(jnp.bfloat16)

    for v in list(range(1, chips)) + [0]:
        start(to_dp(g_part.at[row_block(ahead(v) * 2 + 1 - core)], g_sib.at[v], gs_sems, v, sibling))

    def chip_sum(v):
        to_dp(g_sib.at[v], g_sib.at[v], gs_sems, v, sibling).wait_recv()
        mine = g_part[row_block(ahead(v) * 2 + core), :].astype(jnp.float32)
        g_chip[v] = (mine + g_sib[v].astype(jnp.float32)).astype(jnp.bfloat16)

    for v in list(range(1, chips)) + [0]:
        chip_sum(v)

    ring_forward(x_place, xr_sems, xl_sems)

    def forward(whole, sems, fsems):
        for v in range(1, chips):
            block = whole.at[row_block(behind(v) * 2 + core)]
            to_dp(block, block, sems, v - 1, sibling).wait_recv()
            start(to_dp(block, block, fsems, v, sibling))

    def from_sibling(whole, fsems):
        for v in range(chips):
            block = whole.at[row_block(behind(v) * 2 + 1 - core)]
            to_dp(block, block, fsems, v, sibling).wait_recv()

    forward(w_all, w_sems, w_fsems)
    for v in range(1, chips):
        start(to_dp(g_chip.at[v], g_recv.at[v - 1], gr_sems, v - 1, ahead(v) * 2 + core))
    for v in range(1, chips):
        start(to_dp(own_p, own_p, p_sems, v - 1, ahead(v) * 2 + core))
    start(to_dp(own_p, own_p, p_fsems, 0, sibling))
    from_sibling(w_all, w_fsems)

    def project(source):
        qkv[source, :] = jnp.dot(
            x_all[source, :], w_all[...], preferred_element_type=jnp.float32
        ).astype(jnp.bfloat16)

    @pl.loop(0, seq_count)
    def _(k):
        order = jnp.where(k < rounds, k, jnp.where(k == seq_count - 1, rounds, k + 1))

        @pl.when(k == seq_count - 1)
        def _():
            ring_finish(x_place, xr_sems, xl_sems)

        project(slot_block(seq_behind(order)))

    for k in range(1, seq_count):
        spot = bias_all.at[:, slot_block(seq_behind(k))]
        to_seq(spot, spot, bias_sems, k - 1, s).wait_recv()

    score_scale = LOG2_E / math.sqrt(head_width)

    def attend(query_rows):
        acc[...] = jnp.zeros_like(acc)
        for head in range(heads_here):
            low = (min(offsets) + head * head_width) // LANES * LANES
            high = round_up(max(offsets) + (head + 1) * head_width, LANES)
            columns = lax.broadcasted_iota(jnp.int32, (1, high - low), 1) + (low - head * head_width) - offset
            own = jnp.where((columns >= 0) & (columns < head_width), 1.0, 0.0)
            query = qkv[query_rows, low:high] * own.astype(jnp.bfloat16)
            scores = lax.dot_general(
                query, qkv[:, part + low:part + high], (((1,), (1,)), ((), ())),
                preferred_element_type=jnp.float32,
            )
            scores = scores * score_scale + bias_all[0:1, :]
            exponent = jnp.exp2(scores - jnp.max(scores, axis=1, keepdims=True))
            total = jnp.sum(exponent, axis=1, keepdims=True)
            mixed = jnp.dot(
                exponent.astype(jnp.bfloat16), qkv[:, 2 * part + low:2 * part + high],
                preferred_element_type=jnp.float32,
            )
            acc[:, low:high] += mixed / total * own

    @pl.loop(0, seq_count)
    def _(i):
        target = seq_ahead(i + 1)
        attend(slot_block(target))

        @pl.when(i < seq_count - 1)
        def _():
            ctx_send[i] = acc[...].astype(jnp.bfloat16)
            to_seq(ctx_send.at[i], ctx_all.at[s], c_sems, i, target).start()

        @pl.when(i == seq_count - 1)
        def _():
            ctx_all[s] = acc[...].astype(jnp.bfloat16)

    total = g_chip[0].astype(jnp.float32)
    for v in range(1, chips):
        to_dp(g_recv.at[v - 1], g_recv.at[v - 1], gr_sems, v - 1, sibling).wait_recv()
        total = total + g_recv[v - 1].astype(jnp.float32)
    g_seq[s] = total.astype(jnp.bfloat16)
    ring_start(g_place, ar_sems, al_sems)

    forward(p_all, p_sems, p_fsems)
    from_sibling(p_all, p_fsems)
    for k in range(1, seq_count):
        spot = ctx_all.at[seq_behind(k)]
        to_seq(ctx_send.at[k - 1], spot, c_sems, k - 1, seq_ahead(k)).wait()
    ring_forward(g_place, ar_sems, al_sems)
    half = math.gcd(width, 256)

    @pl.loop(0, width // half)
    def _(j):
        span = pl.ds(pl.multiple_of(j * half, half), half)
        result = pos[:, span]
        for owner in range(seq_count):
            result = result + jnp.dot(
                ctx_all[owner], p_all[starts[owner]:starts[owner] + part, span],
                preferred_element_type=jnp.float32,
            )
        out_ref[:, span] = result.astype(jnp.bfloat16)

    ring_finish(g_place, ar_sems, al_sems)
    total = g_seq[0].astype(jnp.float32)
    for owner in range(1, seq_count):
        total = total + g_seq[owner].astype(jnp.float32)
    grad_ref[...] = total * (1.0 / math.sqrt(dp_count * seq_count * slots))
    for copy in sends:
        copy.wait_send()


def on_device(tokens, tube_index, counts, qkv_weight, proj_weight, ctx_b, cot_b, b_counts):
    slot_cap = tokens.shape[1]
    model_width = tokens.shape[2]
    seq_count = lax.axis_size("seq")
    dp_count = lax.axis_size("dp")
    heads_here = HEADS // seq_count
    head_width = model_width // HEADS
    head_cols = heads_here * head_width
    part, _ = window(model_width, seq_count, head_cols)
    chips = dp_count // 2
    rows = qkv_weight.shape[0]
    rounds = seq_count // 2
    places = jnp.arange(model_width // 2, dtype=jnp.float32)
    frequency = jnp.exp(places * (-2.0 * math.log(10000.0) / model_width))[None, :]
    in_vmem = pl.BlockSpec(memory_space=pltpu.VMEM)
    in_place = pl.BlockSpec(memory_space=pl.ANY)
    bf16, f32 = jnp.bfloat16, jnp.float32
    out_a, weight_grad = pl.pallas_call(
        functools.partial(block_kernel, dp_count, seq_count, heads_here, head_width),
        out_shape=(
            jax.ShapeDtypeStruct((slot_cap, model_width), bf16),
            jax.ShapeDtypeStruct((rows, model_width), f32),
        ),
        in_specs=[in_vmem] * 5 + [in_place] * 4,
        out_specs=(in_vmem, in_vmem),
        scratch_shapes=[
            pltpu.VMEM((seq_count * slot_cap, model_width), bf16),
            pltpu.VMEM((8, seq_count * slot_cap), f32),
            pltpu.VMEM((model_width, 3 * part), bf16),
            pltpu.VMEM((model_width, model_width), bf16),
            pltpu.VMEM((seq_count * slot_cap, 3 * part), bf16),
            pltpu.VMEM((slot_cap, part), f32),
            pltpu.VMEM((seq_count - 1, slot_cap, part), bf16),
            pltpu.VMEM((seq_count, slot_cap, part), bf16),
            pltpu.VMEM((model_width, model_width), bf16),
            pltpu.VMEM((chips, rows, model_width), bf16),
            pltpu.VMEM((chips, rows, model_width), bf16),
            pltpu.VMEM((chips - 1, rows, model_width), bf16),
            pltpu.VMEM((seq_count, rows, model_width), bf16),
            pltpu.VMEM((slot_cap, model_width), f32),
            pltpu.VMEM((slot_cap, 8), f32),
            pltpu.VMEM((slot_cap, model_width), bf16),
            pltpu.VMEM((slot_cap, model_width), bf16),
            pltpu.SemaphoreType.DMA((6,)),
            pltpu.SemaphoreType.DMA((2, rounds, 2)),
            pltpu.SemaphoreType.DMA((2, rounds, 2)),
            pltpu.SemaphoreType.DMA((2, seq_count - 1)),
            pltpu.SemaphoreType.DMA((2, chips - 1)),
            pltpu.SemaphoreType.DMA((2, chips)),
            pltpu.SemaphoreType.DMA((2, chips - 1)),
            pltpu.SemaphoreType.DMA((2, chips)),
            pltpu.SemaphoreType.DMA((2, seq_count - 1)),
            pltpu.SemaphoreType.DMA((2, chips)),
            pltpu.SemaphoreType.DMA((2, chips - 1)),
            pltpu.SemaphoreType.DMA((2, rounds, 2)),
            pltpu.SemaphoreType.DMA((2, rounds, 2)),
        ],
        compiler_params=pltpu.CompilerParams(
            collective_id=0, has_side_effects=True, vmem_limit_bytes=60 * 1024 * 1024
        ),
        name="attention_block",
    )(tokens[0], tube_index, frequency, counts, b_counts, qkv_weight, proj_weight, ctx_b[0], cot_b[0])
    return (out_a[None], weight_grad)


def solution(mesh):
    in_specs = (
        P("dp", "seq", None),
        P("dp", "seq"),
        P("dp", "seq"),
        P("dp", None),
        P("dp", None),
        P("dp", "seq", None),
        P("dp", "seq", None),
        P("dp", "seq"),
    )
    out_specs = (P("dp", "seq", None), P("dp", None))
    return jax.shard_map(
        on_device, mesh=mesh, in_specs=in_specs, out_specs=out_specs, check_vma=False
    )
```

time: 234 us -> 106 us (0.45)
  waiting for transfers between devices: 108 us -> 0 us
  Pallas kernels: 0 us -> 99.1 us
  matrix products: 40.5 us -> 0 us
  local copies, waits for them, and re-layouts: 33.1 us -> 2.93 us
  blocking collectives: 25.7 us -> 0 us
  between operations: 15.2 us -> 1.94 us
  starting transfers between devices: 8.06 us -> 0 us
  other arithmetic: 3.06 us -> 0.6 us
    pallas_call x0 -> x1, Pallas kernels: none -> 99.1 us  [on_device(): pl.pallas_call(functools.partial(block_kernel, dp_count, seq_count, heads...]
    all_gather x2 -> x0, waiting for transfers between devices: 66.3 us -> none  [the longest x1 47.5 us: on_device(): lax.all_gather(qkv_weight, 'dp', axis=0, tiled=True)]
    unnamed x5 -> x0, waiting for transfers between devices: 41.4 us -> none
    dot_general x5 -> x0, matrix products: 26.4 us -> none  [the longest x2 9.71 us: one_block(): jnp.einsum('hqk,khd->qhd', weights, value_rows, preferred_element_type=jn...]
    unnamed x1 -> x0, blocking collectives: 25.7 us -> none
    sub x2 -> x0, matrix products: 14.2 us -> none  [one_block(): exponent = jnp.exp(scores - top_score)]
    unnamed x27 -> x4, local copies, waits for them, and re-layouts: 15.2 us -> 2.93 us
    reshape x1 -> x0, local copies, waits for them, and re-layouts: 11.2 us -> none  [on_device(): projected.reshape(slot_cap, 3, model_width)]
  transfers between devices with their start and end apart: 6 -> 0, of which waited for: 3 -> 0; matrix products, arithmetic and copies ran while one was open for 31% -> 0% of each run, Pallas kernels for 0% -> 0%
where the time goes in v1:
time: 106 us; the launch traced here: 105 us
  Pallas kernels  99.1 us (93%)
  local copies, waits for them, and re-layouts  2.93 us (3%)
  between operations  1.94 us (2%)
    pallas_call x1, Pallas kernels, on_device(): pl.pallas_call(functools.partial(block_kernel, dp_count, seq_count, heads...  99.1 us
    unnamed x4, local copies, waits for them, and re-layouts  2.93 us

profile of v1, /device:TPU:0, one launch (start us, length us, event | category | flops | bytes accessed | tf_op | source)
XLA Modules:
  0.0 104.5 jit_solution(15204163921775283313)
XLA Ops:
  1.9 0.6 multiply_exponential_fusion.freq_ref
  2.5 99.1 %attention_block.1 = (bf16[256,1280]{1,0:T(8,128)(2,1)}, f32[160,1280]{1,0:T(8,128)}) custom-call(bf16[256,1280]{1,0:T(8,128)(2,1)} %bitcast.5, s32[1,256]{1,0:T(1,128)} %index_ref.1, f32[1,640]{1,0:T(1,128)} %multiply_exponential_fusion.freq_ref, s32[1,1]{1,0:T(1,128)S(6)} %copy.12.count_ref, s32[1,1]{1,0:T(1,128)S(6)} %copy.13.bcount_ref, ...), custom_call_target="tpu_custom_call" | custom-call | tf_op jit(solution)/shard_map/attention_block/pallas_call | solution.py:335
  101.6 0.0 copy-start
  101.6 2.0 %copy.14 = bf16[1,256,1280]{2,1,0:T(8,128)(2,1)} copy(bf16[1,256,1280]{2,1,0:T(8,128)(2,1)} %bitcast.4) | data formatting | bytes 1310720
  103.7 0.0 copy-done
  103.7 0.9 copy.15
Async XLA Ops:
  101.6 2.1 %copy-start = (f32[160,1280]{1,0:T(8,128)S(1)}, f32[160,1280]{1,0:T(8,128)}, u32[]{:S(2)}) copy-start(f32[160,1280]{1,0:T(8,128)} %get-tuple-element.9) | copy-start | bytes 2457604

commit v2 on v1

--- a/solution.py
+++ b/solution.py
@@ -37,7 +37,7 @@
     tok_ref, index_ref, freq_ref, count_ref, bcount_ref, w_ref, proj_ref, ctxb_ref, cot_ref,
     out_ref, grad_ref,
     x_all, bias_all, w_all, p_all, qkv, acc, ctx_send, ctx_all,
-    g_part, g_sib, g_chip, g_recv, g_seq, pos, index_col, ctxb, cot,
+    g_part, g_sib, g_chip, g_recv, g_seq, g_in, g_out, pos, index_col, ctxb, cot,
     l_sems, xr_sems, xl_sems, bias_sems, w_sems, w_fsems, p_sems, p_fsems, c_sems, gs_sems, gr_sems,
     ar_sems, al_sems,
 ):
@@ -164,10 +164,6 @@
         half_rows = slots // 2
         return x_all.at[pl.ds(pl.multiple_of(origin * slots + piece * half_rows, half_rows), half_rows)]
 
-    def g_place(origin, piece):
-        half_rows = rows // 2
-        return g_seq.at[origin, pl.ds(piece * half_rows, half_rows)]
-
     own_w = w_all.at[row_block(d)]
     own_p = p_all.at[row_block(d)]
     for v in range(1, chips):
@@ -203,7 +199,6 @@
     for v in list(range(1, chips)) + [0]:
         chip_sum(v)
 
-    ring_forward(x_place, xr_sems, xl_sems)
 
     def forward(whole, sems, fsems):
         for v in range(1, chips):
@@ -222,6 +217,7 @@
     for v in range(1, chips):
         start(to_dp(own_p, own_p, p_sems, v - 1, ahead(v) * 2 + core))
     start(to_dp(own_p, own_p, p_fsems, 0, sibling))
+    ring_forward(x_place, xr_sems, xl_sems)
     from_sibling(w_all, w_fsems)
 
     def project(source):
@@ -242,6 +238,18 @@
     for k in range(1, seq_count):
         spot = bias_all.at[:, slot_block(seq_behind(k))]
         to_seq(spot, spot, bias_sems, k - 1, s).wait_recv()
+
+    for v in range(1, chips):
+        to_dp(g_recv.at[v - 1], g_recv.at[v - 1], gr_sems, v - 1, sibling).wait_recv()
+    piece_rows = rows // seq_count
+    for owner in range(seq_count):
+        span = slice(owner * piece_rows, (owner + 1) * piece_rows)
+        total = g_chip[0, span].astype(jnp.float32)
+        for v in range(1, chips):
+            total = total + g_recv[v - 1, span].astype(jnp.float32)
+        g_seq[owner] = total.astype(jnp.bfloat16)
+    for k in range(1, seq_count):
+        start(to_seq(g_seq.at[seq_ahead(k)], g_in.at[s], ar_sems, k - 1, seq_ahead(k)))
 
     score_scale = LOG2_E / math.sqrt(head_width)
 
@@ -280,19 +288,22 @@
         def _():
             ctx_all[s] = acc[...].astype(jnp.bfloat16)
 
-    total = g_chip[0].astype(jnp.float32)
-    for v in range(1, chips):
-        to_dp(g_recv.at[v - 1], g_recv.at[v - 1], gr_sems, v - 1, sibling).wait_recv()
-        total = total + g_recv[v - 1].astype(jnp.float32)
-    g_seq[s] = total.astype(jnp.bfloat16)
-    ring_start(g_place, ar_sems, al_sems)
+    for k in range(1, seq_count):
+        spot = g_in.at[seq_behind(k)]
+        to_seq(spot, spot, ar_sems, k - 1, s).wait_recv()
+    g_in[s] = g_seq[s]
+    total = g_in[0].astype(jnp.float32)
+    for owner in range(1, seq_count):
+        total = total + g_in[owner].astype(jnp.float32)
+    g_out[s] = total.astype(jnp.bfloat16)
+    for k in range(1, seq_count):
+        start(to_seq(g_out.at[s], g_out.at[s], al_sems, k - 1, seq_ahead(k)))
 
     forward(p_all, p_sems, p_fsems)
     from_sibling(p_all, p_fsems)
     for k in range(1, seq_count):
         spot = ctx_all.at[seq_behind(k)]
         to_seq(ctx_send.at[k - 1], spot, c_sems, k - 1, seq_ahead(k)).wait()
-    ring_forward(g_place, ar_sems, al_sems)
     half = math.gcd(width, 256)
 
     @pl.loop(0, width // half)
@@ -306,11 +317,12 @@
             )
         out_ref[:, span] = result.astype(jnp.bfloat16)
 
-    ring_finish(g_place, ar_sems, al_sems)
-    total = g_seq[0].astype(jnp.float32)
-    for owner in range(1, seq_count):
-        total = total + g_seq[owner].astype(jnp.float32)
-    grad_ref[...] = total * (1.0 / math.sqrt(dp_count * seq_count * slots))
+    for k in range(1, seq_count):
+        spot = g_out.at[seq_behind(k)]
+        to_seq(spot, spot, al_sems, k - 1, s).wait_recv()
+    factor = 1.0 / math.sqrt(dp_count * seq_count * slots)
+    for owner in range(seq_count):
+        grad_ref[owner * piece_rows:(owner + 1) * piece_rows, :] = g_out[owner].astype(jnp.float32) * factor
     for copy in sends:
         copy.wait_send()
 
@@ -353,7 +365,9 @@
             pltpu.VMEM((chips, rows, model_width), bf16),
             pltpu.VMEM((chips, rows, model_width), bf16),
             pltpu.VMEM((chips - 1, rows, model_width), bf16),
-            pltpu.VMEM((seq_count, rows, model_width), bf16),
+            pltpu.VMEM((seq_count, rows // seq_count, model_width), bf16),
+            pltpu.VMEM((seq_count, rows // seq_count, model_width), bf16),
+            pltpu.VMEM((seq_count, rows // seq_count, model_width), bf16),
             pltpu.VMEM((slot_cap, model_width), f32),
             pltpu.VMEM((slot_cap, 8), f32),
             pltpu.VMEM((slot_cap, model_width), bf16),
@@ -369,8 +383,8 @@
             pltpu.SemaphoreType.DMA((2, seq_count - 1)),
             pltpu.SemaphoreType.DMA((2, chips)),
             pltpu.SemaphoreType.DMA((2, chips - 1)),
-            pltpu.SemaphoreType.DMA((2, rounds, 2)),
-            pltpu.SemaphoreType.DMA((2, rounds, 2)),
+            pltpu.SemaphoreType.DMA((2, seq_count - 1)),
+            pltpu.SemaphoreType.DMA((2, seq_count - 1)),
         ],
         compiler_params=pltpu.CompilerParams(
             collective_id=0, has_side_effects=True, vmem_limit_bytes=60 * 1024 * 1024

time: 106 us -> 95.7 us (0.903)
  Pallas kernels: 99.1 us -> 89.8 us
    pallas_call x1, Pallas kernels: 99.1 us -> 89.8 us  [on_device(): pl.pallas_call(functools.partial(block_kernel, dp_count, seq_count, heads...]
where the time goes in v2:
time: 95.7 us; the launch traced here: 95.2 us
  Pallas kernels  89.8 us (94%)
  local copies, waits for them, and re-layouts  2.93 us (3%)
  between operations  1.94 us (2%)
    pallas_call x1, Pallas kernels, on_device(): pl.pallas_call(functools.partial(block_kernel, dp_count, seq_count, heads...  89.8 us
    unnamed x4, local copies, waits for them, and re-layouts  2.93 us

profile of v2, /device:TPU:0, one launch (start us, length us, event | category | flops | bytes accessed | tf_op | source)
XLA Modules:
  0.0 95.2 jit_solution(10792344913266749647)
XLA Ops:
  1.9 0.6 multiply_exponential_fusion.freq_ref
  2.5 89.8 %attention_block.1 = (bf16[256,1280]{1,0:T(8,128)(2,1)}, f32[160,1280]{1,0:T(8,128)}) custom-call(bf16[256,1280]{1,0:T(8,128)(2,1)} %bitcast.5, s32[1,256]{1,0:T(1,128)} %index_ref.1, f32[1,640]{1,0:T(1,128)} %multiply_exponential_fusion.freq_ref, s32[1,1]{1,0:T(1,128)S(6)} %copy.12.count_ref, s32[1,1]{1,0:T(1,128)S(6)} %copy.13.bcount_ref, ...), custom_call_target="tpu_custom_call" | custom-call | tf_op jit(solution)/shard_map/attention_block/pallas_call | solution.py:347
  92.3 0.0 copy-start
  92.3 2.0 %copy.14 = bf16[1,256,1280]{2,1,0:T(8,128)(2,1)} copy(bf16[1,256,1280]{2,1,0:T(8,128)(2,1)} %bitcast.4) | data formatting | bytes 1310720
  94.3 0.0 copy-done
  94.3 0.9 copy.15
Async XLA Ops:
  92.3 2.1 %copy-start = (f32[160,1280]{1,0:T(8,128)S(1)}, f32[160,1280]{1,0:T(8,128)}, u32[]{:S(2)}) copy-start(f32[160,1280]{1,0:T(8,128)} %get-tuple-element.9) | copy-start | bytes 2457604

commit v3 on v1

--- a/solution.py
+++ b/solution.py
@@ -37,9 +37,9 @@
     tok_ref, index_ref, freq_ref, count_ref, bcount_ref, w_ref, proj_ref, ctxb_ref, cot_ref,
     out_ref, grad_ref,
     x_all, bias_all, w_all, p_all, qkv, acc, ctx_send, ctx_all,
-    g_part, g_sib, g_chip, g_recv, g_seq, pos, index_col, ctxb, cot,
+    g_part, g_sib, g_chip, g_recv, g_seq, g_in, g_out, pos, index_col, ctxb, cot,
     l_sems, xr_sems, xl_sems, bias_sems, w_sems, w_fsems, p_sems, p_fsems, c_sems, gs_sems, gr_sems,
-    ar_sems, al_sems,
+    ar_sems, al_sems, ab_sems, ac_sems,
 ):
     d = lax.axis_index("dp")
     s = lax.axis_index("seq")
@@ -130,49 +130,49 @@
         copy.start()
         sends.append(copy)
 
-    right, left = seq_ahead(1), seq_behind(1)
-    rounds = seq_count // 2
-
-    def ring_piece(place, sems, step, origin, piece, target):
-        block = place(origin, piece)
-        return pltpu.make_async_remote_copy(
-            src_ref=block, dst_ref=block, send_sem=sems.at[0, step, piece], recv_sem=sems.at[1, step, piece],
-            device_id={"dp": d, "seq": target}, device_id_type=MESH,
-        )
-
-    def ring_start(place, r_sems, l_sems):
-        for order in range(2):
-            if order == 0 or rounds > 1:
-                start(ring_piece(place, r_sems, 0, s, order, right))
-                start(ring_piece(place, l_sems, 0, s, 1 - order, left))
-
-    def ring_forward(place, r_sems, l_sems):
-        for step in range(1, rounds):
-            for order in range(2):
-                ring_piece(place, r_sems, step - 1, seq_behind(step), order, right).wait_recv()
-                if order == 0 or step < rounds - 1:
-                    start(ring_piece(place, r_sems, step, seq_behind(step), order, right))
-                ring_piece(place, l_sems, step - 1, seq_ahead(step), 1 - order, left).wait_recv()
-                if order == 0 or step < rounds - 1:
-                    start(ring_piece(place, l_sems, step, seq_ahead(step), 1 - order, left))
-
-    def ring_finish(place, r_sems, l_sems):
-        ring_piece(place, r_sems, rounds - 1, seq_behind(rounds), 0, right).wait_recv()
-        ring_piece(place, l_sems, rounds - 1, seq_ahead(rounds), 1, left).wait_recv()
-
-    def x_place(origin, piece):
-        half_rows = slots // 2
-        return x_all.at[pl.ds(pl.multiple_of(origin * slots + piece * half_rows, half_rows), half_rows)]
-
-    def g_place(origin, piece):
-        half_rows = rows // 2
-        return g_seq.at[origin, pl.ds(piece * half_rows, half_rows)]
+    last_hop = seq_count - 2
+
+    def line_copy(side, hop, origin):
+        block = x_all.at[slot_block(lax.rem(origin + 2 * seq_count, seq_count))]
+        sems = xr_sems if side > 0 else xl_sems
+        target = lax.rem(s + side + seq_count, seq_count)
+        return to_seq(block, block, sems, hop, target)
+
+    def line_sends(side, hop):
+        origin = s - side * hop
+        neighbour = s + side
+        return (origin >= 0) & (origin < seq_count) & (neighbour >= 0) & (neighbour < seq_count)
+
+    def line_start(hop):
+        for side in (1, -1):
+            @pl.when(line_sends(side, hop))
+            def _():
+                line_copy(side, hop, s - side * hop).start()
+
+    def line_arrive(hop):
+        for side in (1, -1):
+            origin = s - side * (hop + 1)
+
+            @pl.when((origin >= 0) & (origin < seq_count))
+            def _():
+                line_copy(side, hop, origin).wait_recv()
+
+    def line_pass(hop):
+        line_arrive(hop - 1)
+        line_start(hop)
+
+    def line_sent():
+        for hop in range(last_hop + 1):
+            for side in (1, -1):
+                @pl.when(line_sends(side, hop))
+                def _():
+                    line_copy(side, hop, s - side * hop).wait_send()
 
     own_w = w_all.at[row_block(d)]
     own_p = p_all.at[row_block(d)]
     for v in range(1, chips):
         start(to_dp(own_w, own_w, w_sems, v - 1, ahead(v) * 2 + core))
-    ring_start(x_place, xr_sems, xl_sems)
+    line_start(0)
     start(to_dp(own_w, own_w, w_fsems, 0, sibling))
     for k in range(1, seq_count):
         spot = bias_all.at[:, slot_block(s)]
@@ -203,7 +203,6 @@
     for v in list(range(1, chips)) + [0]:
         chip_sum(v)
 
-    ring_forward(x_place, xr_sems, xl_sems)
 
     def forward(whole, sems, fsems):
         for v in range(1, chips):
@@ -216,6 +215,8 @@
             block = whole.at[row_block(behind(v) * 2 + 1 - core)]
             to_dp(block, block, fsems, v, sibling).wait_recv()
 
+    if last_hop >= 1:
+        line_pass(1)
     forward(w_all, w_sems, w_fsems)
     for v in range(1, chips):
         start(to_dp(g_chip.at[v], g_recv.at[v - 1], gr_sems, v - 1, ahead(v) * 2 + core))
@@ -223,6 +224,30 @@
         start(to_dp(own_p, own_p, p_sems, v - 1, ahead(v) * 2 + core))
     start(to_dp(own_p, own_p, p_fsems, 0, sibling))
     from_sibling(w_all, w_fsems)
+    for hop in range(2, last_hop + 1):
+        line_pass(hop)
+
+    half_rows = rows // 2
+    owners = (seq_count // 2 - 1, seq_count // 2)
+
+    def grad_copy(half, sender):
+        return pltpu.make_async_remote_copy(
+            src_ref=g_seq.at[half], dst_ref=g_in.at[sender], send_sem=ar_sems.at[half], recv_sem=al_sems.at[sender],
+            device_id={"dp": d, "seq": owners[half]}, device_id_type=MESH,
+        )
+
+    for v in range(1, chips):
+        to_dp(g_recv.at[v - 1], g_recv.at[v - 1], gr_sems, v - 1, sibling).wait_recv()
+    for half in range(2):
+        span = slice(half * half_rows, (half + 1) * half_rows)
+        total = g_chip[0, span].astype(jnp.float32)
+        for v in range(1, chips):
+            total = total + g_recv[v - 1, span].astype(jnp.float32)
+        g_seq[half] = total.astype(jnp.bfloat16)
+
+        @pl.when(s != owners[half])
+        def _():
+            grad_copy(half, s).start()
 
     def project(source):
         qkv[source, :] = jnp.dot(
@@ -231,13 +256,11 @@
 
     @pl.loop(0, seq_count)
     def _(k):
-        order = jnp.where(k < rounds, k, jnp.where(k == seq_count - 1, rounds, k + 1))
-
         @pl.when(k == seq_count - 1)
         def _():
-            ring_finish(x_place, xr_sems, xl_sems)
-
-        project(slot_block(seq_behind(order)))
+            line_arrive(last_hop)
+
+        project(slot_block(jnp.where(s == seq_count - 1, seq_behind(k), seq_ahead(k))))
 
     for k in range(1, seq_count):
         spot = bias_all.at[:, slot_block(seq_behind(k))]
@@ -266,6 +289,12 @@
             )
             acc[:, low:high] += mixed / total * own
 
+    def at_end(index):
+        return (index == 0) | (index == seq_count - 1)
+
+    def ctx_copy(i):
+        return to_seq(ctx_send.at[i], ctx_all.at[s], c_sems, i, seq_ahead(i + 1))
+
     @pl.loop(0, seq_count)
     def _(i):
         target = seq_ahead(i + 1)
@@ -274,25 +303,48 @@
         @pl.when(i < seq_count - 1)
         def _():
             ctx_send[i] = acc[...].astype(jnp.bfloat16)
-            to_seq(ctx_send.at[i], ctx_all.at[s], c_sems, i, target).start()
+
+            @pl.when(jnp.logical_not(at_end(target)))
+            def _():
+                ctx_copy(i).start()
 
         @pl.when(i == seq_count - 1)
         def _():
             ctx_all[s] = acc[...].astype(jnp.bfloat16)
 
-    total = g_chip[0].astype(jnp.float32)
-    for v in range(1, chips):
-        to_dp(g_recv.at[v - 1], g_recv.at[v - 1], gr_sems, v - 1, sibling).wait_recv()
-        total = total + g_recv[v - 1].astype(jnp.float32)
-    g_seq[s] = total.astype(jnp.bfloat16)
-    ring_start(g_place, ar_sems, al_sems)
+    for half in range(2):
+        @pl.when(s == owners[half])
+        def _():
+            for k in range(1, seq_count):
+                grad_copy(half, seq_behind(k)).wait_recv()
+            g_in[s] = g_seq[half]
+            total = g_in[0].astype(jnp.float32)
+            for sender in range(1, seq_count):
+                total = total + g_in[sender].astype(jnp.float32)
+            g_out[half] = total.astype(jnp.bfloat16)
+
+    def grad_back(half, k):
+        return pltpu.make_async_remote_copy(
+            src_ref=g_out.at[half], dst_ref=g_out.at[half], send_sem=ab_sems.at[k - 1],
+            recv_sem=ac_sems.at[half], device_id={"dp": d, "seq": seq_ahead(k)}, device_id_type=MESH,
+        )
+
+    line_sent()
+    for k in range(1, seq_count):
+        @pl.when(at_end(seq_ahead(k)))
+        def _():
+            ctx_copy(k - 1).start()
+    for half in range(2):
+        @pl.when(s == owners[half])
+        def _():
+            for k in range(1, seq_count):
+                grad_back(half, k).start()
 
     forward(p_all, p_sems, p_fsems)
     from_sibling(p_all, p_fsems)
     for k in range(1, seq_count):
         spot = ctx_all.at[seq_behind(k)]
         to_seq(ctx_send.at[k - 1], spot, c_sems, k - 1, seq_ahead(k)).wait()
-    ring_forward(g_place, ar_sems, al_sems)
     half = math.gcd(width, 256)
 
     @pl.loop(0, width // half)
@@ -306,11 +358,20 @@
             )
         out_ref[:, span] = result.astype(jnp.bfloat16)
 
-    ring_finish(g_place, ar_sems, al_sems)
-    total = g_seq[0].astype(jnp.float32)
-    for owner in range(1, seq_count):
-        total = total + g_seq[owner].astype(jnp.float32)
-    grad_ref[...] = total * (1.0 / math.sqrt(dp_count * seq_count * slots))
+    for half in range(2):
+        @pl.when(s != owners[half])
+        def _():
+            grad_back(half, 1).wait_recv()
+            grad_copy(half, s).wait_send()
+
+        @pl.when(s == owners[half])
+        def _():
+            for k in range(1, seq_count):
+                grad_back(half, k).wait_send()
+
+    factor = 1.0 / math.sqrt(dp_count * seq_count * slots)
+    for half in range(2):
+        grad_ref[half * half_rows:(half + 1) * half_rows, :] = g_out[half].astype(jnp.float32) * factor
     for copy in sends:
         copy.wait_send()
 
@@ -326,7 +387,6 @@
     part, _ = window(model_width, seq_count, head_cols)
     chips = dp_count // 2
     rows = qkv_weight.shape[0]
-    rounds = seq_count // 2
     places = jnp.arange(model_width // 2, dtype=jnp.float32)
     frequency = jnp.exp(places * (-2.0 * math.log(10000.0) / model_width))[None, :]
     in_vmem = pl.BlockSpec(memory_space=pltpu.VMEM)
@@ -353,14 +413,16 @@
             pltpu.VMEM((chips, rows, model_width), bf16),
             pltpu.VMEM((chips, rows, model_width), bf16),
             pltpu.VMEM((chips - 1, rows, model_width), bf16),
-            pltpu.VMEM((seq_count, rows, model_width), bf16),
+            pltpu.VMEM((2, rows // 2, model_width), bf16),
+            pltpu.VMEM((seq_count, rows // 2, model_width), bf16),
+            pltpu.VMEM((2, rows // 2, model_width), bf16),
             pltpu.VMEM((slot_cap, model_width), f32),
             pltpu.VMEM((slot_cap, 8), f32),
             pltpu.VMEM((slot_cap, model_width), bf16),
             pltpu.VMEM((slot_cap, model_width), bf16),
             pltpu.SemaphoreType.DMA((6,)),
-            pltpu.SemaphoreType.DMA((2, rounds, 2)),
-            pltpu.SemaphoreType.DMA((2, rounds, 2)),
+            pltpu.SemaphoreType.DMA((2, seq_count - 1)),
+            pltpu.SemaphoreType.DMA((2, seq_count - 1)),
             pltpu.SemaphoreType.DMA((2, seq_count - 1)),
             pltpu.SemaphoreType.DMA((2, chips - 1)),
             pltpu.SemaphoreType.DMA((2, chips)),
@@ -369,8 +431,10 @@
             pltpu.SemaphoreType.DMA((2, seq_count - 1)),
             pltpu.SemaphoreType.DMA((2, chips)),
             pltpu.SemaphoreType.DMA((2, chips - 1)),
-            pltpu.SemaphoreType.DMA((2, rounds, 2)),
-            pltpu.SemaphoreType.DMA((2, rounds, 2)),
+            pltpu.SemaphoreType.DMA((2,)),
+            pltpu.SemaphoreType.DMA((seq_count,)),
+            pltpu.SemaphoreType.DMA((seq_count - 1,)),
+            pltpu.SemaphoreType.DMA((2,)),
         ],
         compiler_params=pltpu.CompilerParams(
             collective_id=0, has_side_effects=True, vmem_limit_bytes=60 * 1024 * 1024

time: 106 us -> 90 us (0.85)
  Pallas kernels: 99.1 us -> 83.8 us
    pallas_call x1, Pallas kernels: 99.1 us -> 83.8 us  [on_device(): pl.pallas_call(functools.partial(block_kernel, dp_count, seq_count, heads...]
where the time goes in v3:
time: 90 us; the launch traced here: 89.3 us
  Pallas kernels  83.8 us (93%)
  local copies, waits for them, and re-layouts  2.93 us (3%)
  between operations  1.94 us (2%)
    pallas_call x1, Pallas kernels, on_device(): pl.pallas_call(functools.partial(block_kernel, dp_count, seq_count, heads...  83.8 us
    unnamed x4, local copies, waits for them, and re-layouts  2.93 us

profile of v3, /device:TPU:0, one launch (start us, length us, event | category | flops | bytes accessed | tf_op | source)
XLA Modules:
  0.0 89.3 jit_solution(2982346278434076283)
XLA Ops:
  1.9 0.6 multiply_exponential_fusion.freq_ref
  2.5 83.8 %attention_block.1 = (bf16[256,1280]{1,0:T(8,128)(2,1)}, f32[160,1280]{1,0:T(8,128)}) custom-call(bf16[256,1280]{1,0:T(8,128)(2,1)} %bitcast.5, s32[1,256]{1,0:T(1,128)} %index_ref.1, f32[1,640]{1,0:T(1,128)} %multiply_exponential_fusion.freq_ref, s32[1,1]{1,0:T(1,128)S(6)} %copy.12.count_ref, s32[1,1]{1,0:T(1,128)S(6)} %copy.13.bcount_ref, ...), custom_call_target="tpu_custom_call" | custom-call | tf_op jit(solution)/shard_map/attention_block/pallas_call | solution.py:395
  86.3 0.0 copy-start
  86.4 2.0 %copy.14 = bf16[1,256,1280]{2,1,0:T(8,128)(2,1)} copy(bf16[1,256,1280]{2,1,0:T(8,128)(2,1)} %bitcast.4) | data formatting | bytes 1310720
  88.4 0.0 copy-done
  88.4 0.9 copy.15
Async XLA Ops:
  86.3 2.1 %copy-start = (f32[160,1280]{1,0:T(8,128)S(1)}, f32[160,1280]{1,0:T(8,128)}, u32[]{:S(2)}) copy-start(f32[160,1280]{1,0:T(8,128)} %get-tuple-element.9) | copy-start | bytes 2457604
